TPU v7x, 32 devices: a whole 2x2x4 slice. The times are simulated.
32 devices in a mesh: branch: 2 (over core), dap: 4 (over z), rep: 4 (over y, x).
Axes of the slice: x: 2, y: 2, z: 4, core: 2. Of those that a mesh axis runs over, the one named last changes fastest.
Arguments:
- homolog_stack: bfloat16 [512, 32, 256], P(('rep', 'branch', 'dap')), parts along dimension 0, may hold values from -6 to 6
- homolog_validity_flags: int32 [512], P(('rep', 'branch', 'dap')), parts along dimension 0, may hold values 0 or 1
- amino_validity_flags: int32 [128], P('rep'), parts along dimension 0, may hold values from 0 to 1, as said below
- offset_classes: int32 [128, 32], P(('rep', 'branch', 'dap')), parts along dimension 0, may hold values from 0 to 65
- couple_matrix: bfloat16 [128, 32, 128], P(('rep', 'branch', 'dap')), parts along dimension 0, may hold values from -6 to 6
- homolog_standardizer_factor: float32 [256], replicated, may hold values from 0.25 to 1.75
- first_factor_projector: bfloat16 [256, 32], replicated, may hold values from -0.375 to 0.375
- second_factor_projector: bfloat16 [256, 32], replicated, may hold values from -0.375 to 0.375
- product_final_projector: bfloat16 [1024, 128], replicated, may hold values from -0.1875 to 0.1875
- offset_embedding_matrix: bfloat16 [66, 128], replicated, may hold values from -6 to 6
- couple_standardizer_factor: float32 [128], replicated, may hold values from 0.25 to 1.75
- trilateral_edge_projectors: bfloat16 [128, 512], replicated, may hold values from -0.5 to 0.5
- trilateral_sigmoid_projector: bfloat16 [128, 128], replicated, may hold values from -0.5 to 0.5
- trilateral_final_projector: bfloat16 [128, 128], replicated, may hold values from -0.5 to 0.5
- trilateral_standardizer_factor: float32 [128], replicated, may hold values from 0.25 to 1.75
Outputs:
- pair_out: bfloat16 [128, 32, 128], P(('rep', 'branch', 'dap')), parts along dimension 0
There are 4 independent parts, one for each index of `rep`. A program takes and returns all parts, laid end to end along the dimension named above; an argument that names none is the same for every part. Nothing has to cross between parts.
Inputs may be any that keep to these rules, and one draw needn't show every extreme that they name: `amino_validity_flags`: 0 or 1; exactly 12 residues are 0, at any positions.
All inputs are finite; a program needn't handle non-finite values. No bound on the sum of `homolog_validity_flags` on one device may be relied on, other than what follows from the above.
Results may differ from a plain program's by a relative error of at most 0.0036.
Values may be sent and summed in bfloat16 or wider, within the bound.
A program may use at most 64 MiB of HBM per device.

v0:
```python
import jax
import jax.numpy as jnp
from jax import lax
from jax.sharding import PartitionSpec as P


def standardize_features(values, gain):
    mean = jnp.mean(values, axis=-1, keepdims=True)
    centred = values - mean
    spread = jnp.mean(centred * centred, axis=-1, keepdims=True)
    return centred * lax.rsqrt(spread + 1e-05) * gain


def on_device(
    homolog_stack,
    homolog_validity_flags,
    amino_validity_flags,
    offset_classes,
    couple_matrix,
    homolog_standardizer_factor,
    first_factor_projector,
    second_factor_projector,
    product_final_projector,
    offset_embedding_matrix,
    couple_standardizer_factor,
    trilateral_edge_projectors,
    trilateral_sigmoid_projector,
    trilateral_final_projector,
    trilateral_standardizer_factor,
):
    plain_real_kind = jnp.float32
    brain_float_half = jnp.bfloat16
    rows_here = couple_matrix.shape[0]
    amino_total = couple_matrix.shape[1]
    width = couple_matrix.shape[2]
    inner = first_factor_projector.shape[1]
    shard_homologs = homolog_stack.shape[0]
    first = lax.axis_index(("branch", "dap")) * rows_here
    standardized_source = standardize_features(
        homolog_stack.astype(plain_real_kind), homolog_standardizer_factor
    ).astype(brain_float_half)
    res_all = amino_validity_flags.astype(plain_real_kind)
    live = homolog_validity_flags.astype(plain_real_kind)[:, None] * res_all[None, :]
    sides = jnp.dot(
        standardized_source.reshape(shard_homologs * amino_total, homolog_stack.shape[2]),
        jnp.concatenate([first_factor_projector, second_factor_projector], axis=1),
        preferred_element_type=plain_real_kind,
    )
    sides = sides.reshape(shard_homologs, amino_total, 2 * inner) * live[:, :, None]
    left_side = sides[..., :inner].astype(brain_float_half)
    right_side = sides[..., inner:].astype(brain_float_half)
    row_flags = homolog_validity_flags.astype(brain_float_half)
    left_rows = lax.all_to_all(
        left_side, ("branch", "dap"), split_axis=1, concat_axis=0, tiled=True
    )
    outer = jnp.einsum(
        "sic,sje->ijce",
        left_rows,
        lax.all_gather(right_side, ("branch", "dap"), axis=0, tiled=True),
        preferred_element_type=plain_real_kind,
    )
    outer, live_rows = (
        outer,
        jnp.sum(
            lax.all_gather(row_flags, ("branch", "dap"), axis=0, tiled=True).astype(plain_real_kind)
        ),
    )
    projected = jnp.dot(
        outer.reshape(rows_here * amino_total, inner * inner),
        product_final_projector.astype(plain_real_kind),
        precision=lax.Precision.HIGHEST,
    ).reshape(rows_here, amino_total, width)
    res_rows = lax.dynamic_slice_in_dim(res_all, first, rows_here, 0)
    pair_live = res_rows[:, None] * res_all[None, :]
    count = jnp.maximum(live_rows * pair_live, 1.0)
    onehot = (
        offset_classes[..., None] == jnp.arange(offset_embedding_matrix.shape[0], dtype=jnp.int32)
    ).astype(brain_float_half)
    embed = jnp.dot(
        onehot.reshape(rows_here * amino_total, offset_embedding_matrix.shape[0]),
        offset_embedding_matrix,
        preferred_element_type=plain_real_kind,
    ).reshape(rows_here, amino_total, width)
    updated = couple_matrix.astype(plain_real_kind) + embed + projected / count[..., None]
    normed_pair = standardize_features(updated, couple_standardizer_factor).astype(brain_float_half)
    flat_pair = normed_pair.reshape(rows_here * amino_total, width)
    four = jnp.dot(
        flat_pair, trilateral_edge_projectors, preferred_element_type=plain_real_kind
    ).reshape(rows_here, amino_total, 4 * width)
    tri_left = (
        jax.nn.sigmoid(four[..., :width]) * four[..., width : 2 * width] * pair_live[..., None]
    ).astype(brain_float_half)
    tri_right = (
        jax.nn.sigmoid(four[..., 2 * width : 3 * width])
        * four[..., 3 * width :]
        * pair_live[..., None]
    ).astype(brain_float_half)
    triangle = jnp.einsum(
        "ikc,jkc->ijc",
        tri_left,
        lax.all_gather(tri_right, ("branch", "dap"), axis=0, tiled=True),
        preferred_element_type=plain_real_kind,
    )
    triangle_normed = standardize_features(triangle, trilateral_standardizer_factor).astype(
        brain_float_half
    )
    gate = jax.nn.sigmoid(
        jnp.dot(flat_pair, trilateral_sigmoid_projector, preferred_element_type=plain_real_kind)
    ).reshape(rows_here, amino_total, width)
    change = jnp.dot(
        triangle_normed.reshape(rows_here * amino_total, width),
        trilateral_final_projector,
        preferred_element_type=plain_real_kind,
    ).reshape(rows_here, amino_total, width)
    return (updated + gate * change).astype(brain_float_half)


def solution(mesh):
    placed = (
        P(("rep", "branch", "dap"), None, None),
        P(("rep", "branch", "dap")),
        P("rep"),
        P(("rep", "branch", "dap"), None),
        P(("rep", "branch", "dap"), None, None),
        P(),
        P(),
        P(),
        P(),
        P(),
        P(),
        P(),
        P(),
        P(),
        P(),
    )
    return jax.shard_map(
        on_device,
        mesh=mesh,
        in_specs=placed,
        out_specs=P(("rep", "branch", "dap"), None, None),
        check_vma=False,
    )
```

profile of v0, /device:TPU:0, one launch (start us, length us, event | category | flops | bytes accessed | tf_op | source)
XLA Modules:
  0.0 97.8 jit_solution(11911952278846096481)
XLA Ops:
  0.0 0.0 copy-start
  0.0 0.0 copy-start.9
  0.0 0.0 copy-start.5
  0.0 0.0 copy-start.2
  0.0 0.0 copy-start.4
  0.0 0.7 convert_element_type.44
  0.7 0.7 fusion.40
  1.5 1.1 %convert_reduce_fusion = f32[16,32]{1,0:T(8,128)S(1)} fusion(bf16[16,32,256]{2,1,0:T(8,128)(2,1)} %param.15), kind=kLoop, calls=%fused_computation.15 | loop fusion | flops 261632 | bytes 264192 | tf_op jit(solution)/shard_map/reduce_sum | solution.py:8
  2.6 1.2 %fusion.10 = f32[16,32]{1,0:T(8,128)S(1)} fusion(bf16[16,32,256]{2,1,0:T(8,128)(2,1)} %param.15, f32[16,32]{1,0:T(8,128)S(1)} %broadcast_multiply_fusion.1), kind=kLoop, calls=%fused_computation.18 | loop fusion | flops 523776 | bytes 266240 | tf_op jit(solution)/shard_map/reduce_sum | solution.py:10
  3.8 0.1 broadcast_multiply_fusion
  3.9 1.3 %fusion = bf16[16,32,64]{2,1,0:T(8,128)(2,1)S(1)} fusion(bf16[16,32,256]{2,1,0:T(8,128)(2,1)} %param.15, f32[256]{0:T(256)} %param.20, f32[16,32]{1,0:T(8,128)S(1)} %add_rsqrt_fusion, f32[16,32]{1,0:T(8,128)S(1)} %broadcast_multiply_fusion.1, f32[16,32]{1,0:T(8,128)S(1)} %broadcast_multiply_fusion, bf16[256,32]{0,1:T(8,128)(2,1)} %param.22, ...), kind=kOutput, calls=%fused_computation.2 | convolution fusion | flops 17563648 | bytes 367616 | tf_op jit(solution)/shard_map/dot_general | solution.py:44
  5.1 0.1 fusion.39
  5.3 0.1 copy.52
  5.3 0.8 reshape.164
  6.1 6.4 %all-to-all-start = ((bf16[8,2,1024]{2,1,0:T(2,128)(2,1)}), bf16[8,2,1024]{2,1,0:T(2,128)(2,1)S(1)}, u32[]{:S(2)}, u32[]{:S(2)}) async-start(bf16[8,2,1024]{2,1,0:T(2,128)(2,1)} %reshape.164), calls=%async_computation | async-start | bytes 65536 | tf_op jit(solution)/shard_map/all_to_all | solution.py:53
  12.5 0.1 dynamic_slice.3
  12.5 0.0 copy-done.9
  12.5 0.7 dynamic-slice
  13.9 0.2 dynamic-update-slice
  14.2 17.2 %all-reduce = bf16[128]{0:T(256)(128)(2,1)S(1)} all-reduce(bf16[128]{0:T(256)(128)(2,1)S(1)} %dynamic-update-slice), channel_id=1, replica_groups=mesh['branch'=2,'dap'=4,'rep'=4] {'branch','dap'}, use_global_device_ids=true, to_apply=%add | all-reduce | flops 128 | bytes 512
  31.4 0.7 convert_reduce_fusion.1
  32.0 0.8 broadcast_multiply_fusion.4
  32.8 0.0 copy-done.5
  32.8 0.0 copy-done.2
  32.8 0.0 copy-done.4
  32.8 0.2 convolution_add_fusion
  33.0 29.4 %all_gather.9 = bf16[128,32,32]{2,1,0:T(8,128)(2,1)S(1)} all-gather(bf16[16,32,32]{2,1,0:T(8,128)(2,1)S(1)} %get-tuple-element.7), channel_id=1, replica_groups=mesh['branch'=2,'dap'=4,'rep'=4] {'branch','dap'}, dimensions={0}, use_global_device_ids=true | all-gather | bytes 294912 | tf_op jit(solution)/shard_map/all_gather | solution.py:59
  62.4 0.0 all-to-all-done
  62.4 0.1 reshape.165
  62.6 2.1 %convolution_bitcast_fusion = f32[4,32,32,32]{2,3,0,1:T(8,128)} fusion(bf16[128,4,32,1]{2,0,1,3:T(8,128)(2,1)S(1)} %bitcast.51, bf16[128,32,32,1]{2,1,0,3:T(8,128)(2,1)S(1)} %bitcast.50), kind=kOutput, calls=%fused_computation | convolution fusion | flops 33554432 | bytes 819200 | tf_op jit(solution)/shard_map/sic,sje->ijce/dot_general | solution.py:56
  64.7 1.9 %copy.40 = f32[4,32,32,32]{3,2,1,0:T(8,128)S(1)} copy(f32[4,32,32,32]{2,3,0,1:T(8,128)} %convolution_bitcast_fusion) | data formatting | bytes 1048576 | tf_op jit(solution)/shard_map/sic,sje->ijce/transpose | solution.py:56
  66.6 0.0 copy-start.6
  66.6 0.0 copy-start.1
  66.6 1.0 dot_general.29
  67.6 0.0 copy-done
  67.6 0.5 fusion.41
  68.1 0.2 multiply_reduce_fusion.1
  68.2 0.0 copy-done.6
  68.3 0.1 multiply_convert_fusion.1
  68.4 0.0 copy-done.1
  68.4 0.2 fusion.18
  68.5 0.0 copy-start.8
  68.6 0.0 copy-start.3
  68.6 0.0 copy-start.7
  68.6 0.1 fusion.21
  68.7 25.4 %all_gather.11 = bf16[32,32,128]{2,1,0:T(8,128)(2,1)S(1)} all-gather(bf16[4,32,128]{2,1,0:T(8,128)(2,1)S(1)} %get-tuple-element.6), channel_id=1, replica_groups=mesh['branch'=2,'dap'=4,'rep'=4] {'branch','dap'}, dimensions={0}, use_global_device_ids=true | all-gather | bytes 294912 | tf_op jit(solution)/shard_map/all_gather | solution.py:101
  94.1 1.4 %copy.41 = bf16[32,32,128]{1,0,2:T(8,128)(2,1)S(1)} copy(bf16[32,32,128]{2,1,0:T(8,128)(2,1)S(1)} %all_gather.11) | data formatting | bytes 524288 | tf_op jit(solution)/shard_map/all_gather | solution.py:101
  95.5 0.1 copy.42
  95.7 0.6 fusion.42
  96.3 0.1 copy.43
  96.4 0.1 bitcast_reduce_fusion
  96.5 0.2 multiply_reduce_fusion
  96.7 0.0 copy-done.8
  96.7 0.2 fusion.4
  96.9 0.0 copy-done.3
  96.9 0.0 copy-done.7
  96.9 0.8 fusion.6
  (8 shorter events, 0.0 us)
Async XLA Ops:
  0.0 67.6 %copy-start = (bf16[1024,128]{1,0:T(8,128)(2,1)S(1)}, bf16[1024,128]{1,0:T(8,128)(2,1)}, u32[]{:S(2)}) copy-start(bf16[1024,128]{1,0:T(8,128)(2,1)} %param.23) | copy-start | bytes 786436
  0.0 12.5 %copy-start.9 = (u32[32]{0:T(128)S(1)}, u32[32]{0:T(128)}, u32[]{:S(2)}) copy-start(u32[32]{0:T(128)} %constant.42) | copy-start | bytes 388
  0.0 32.8 %copy-start.5 = (s32[4,32]{1,0:T(4,128)S(1)}, s32[4,32]{1,0:T(4,128)}, u32[]{:S(2)}) copy-start(s32[4,32]{1,0:T(4,128)} %param.18) | copy-start | bytes 1540
  0.0 32.8 %copy-start.2 = (bf16[4,32,128]{2,1,0:T(8,128)(2,1)S(1)}, bf16[4,32,128]{2,1,0:T(8,128)(2,1)}, u32[]{:S(2)}) copy-start(bf16[4,32,128]{2,1,0:T(8,128)(2,1)} %param.19) | copy-start | bytes 98308
  0.0 32.8 %copy-start.4 = (bf16[66,128]{1,0:T(8,128)(2,1)S(1)}, bf16[66,128]{1,0:T(8,128)(2,1)}, u32[]{:S(2)}) copy-start(bf16[66,128]{1,0:T(8,128)(2,1)} %param.24) | copy-start | bytes 50692
  6.1 56.3 %all-to-all-start = ((bf16[8,2,1024]{2,1,0:T(2,128)(2,1)}), bf16[8,2,1024]{2,1,0:T(2,128)(2,1)S(1)}, u32[]{:S(2)}, u32[]{:S(2)}) async-start(bf16[8,2,1024]{2,1,0:T(2,128)(2,1)} %reshape.164), calls=%async_computation | async-start | bytes 65536 | tf_op jit(solution)/shard_map/all_to_all | solution.py:53
  66.6 1.6 %copy-start.6 = (f32[128]{0:T(128)S(1)}, f32[128]{0:T(128)}, u32[]{:S(2)}) copy-start(f32[128]{0:T(128)} %param.25) | copy-start | bytes 1540
  66.6 1.7 %copy-start.1 = (bf16[128,512]{1,0:T(8,128)(2,1)S(1)}, bf16[128,512]{1,0:T(8,128)(2,1)}, u32[]{:S(2)}) copy-start(bf16[128,512]{1,0:T(8,128)(2,1)} %param.26) | copy-start | bytes 393220
  68.5 28.2 %copy-start.8 = (bf16[128,128]{1,0:T(8,128)(2,1)S(1)}, bf16[128,128]{1,0:T(8,128)(2,1)}, u32[]{:S(2)}) copy-start(bf16[128,128]{1,0:T(8,128)(2,1)} %param.27) | copy-start | bytes 98308
  68.6 28.3 %copy-start.3 = (bf16[128,128]{1,0:T(8,128)(2,1)S(1)}, bf16[128,128]{1,0:T(8,128)(2,1)}, u32[]{:S(2)}) copy-start(bf16[128,128]{1,0:T(8,128)(2,1)} %param.28) | copy-start | bytes 98308
  68.6 28.3 %copy-start.7 = (f32[128]{0:T(128)S(1)}, f32[128]{0:T(128)}, u32[]{:S(2)}) copy-start(f32[128]{0:T(128)} %param.29) | copy-start | bytes 1540
where the time goes:
time: 98.2 us; the launch traced here: 97.8 us
  blocking collectives  72 us (73%)
  local copies, waits for them, and re-layouts  6.71 us (7%)
  starting transfers between devices  6.36 us (6%)
  other arithmetic  5.91 us (6%)
  matrix products  5.8 us (6%)
    all_gather x1, blocking collectives, on_device(): lax.all_gather(right_side, ('branch', 'dap'), axis=0, tiled=True)  29.4 us
    all_gather x1, blocking collectives, on_device(): lax.all_gather(tri_right, ('branch', 'dap'), axis=0, tiled=True)  25.4 us
    unnamed x1, blocking collectives  17.2 us
    all_to_all x1, starting transfers between devices, on_device(): lax.all_to_all(left_side, ('branch', 'dap'), split_axis=1, concat_axis=0,...  6.36 us
    dot_general x1, matrix products, on_device(): jnp.einsum('sic,sje->ijce', left_rows, lax.all_gather(right_side, ('branc...  2.08 us
  transfers between devices with their start and end apart: 1, of which 0 were waited for; matrix products, arithmetic and copies ran while one was open for 3% of the time, Pallas kernels for 0%

commit v1 on v0

v1 whole, which is shorter than its diff:
```python
import functools

import jax
import jax.numpy as jnp
from jax import lax
from jax.experimental import pallas as pl
from jax.experimental.pallas import tpu as pltpu
from jax.sharding import PartitionSpec as P

F32 = jnp.float32
BF16 = jnp.bfloat16
MESH = pl.DeviceIdType.MESH
LANES = 128
SUB = 8


def iota(shape, axis):
    return lax.broadcasted_iota(jnp.int32, shape, axis)


def dot(a, b):
    return jnp.dot(a, b, preferred_element_type=F32)


def standardize(values, gain):
    mean = jnp.mean(values, axis=-1, keepdims=True)
    centred = values - mean
    spread = jnp.mean(centred * centred, axis=-1, keepdims=True)
    return centred * lax.rsqrt(spread + 1e-05) * gain


def kernel(
    nb, nz,
    x_ref, hflag_ref, aflag_ref, class_ref, couple_ref, hgain_ref, wl_ref, wr_ref, wout_ref,
    embed_ref, cgain_ref, wedge_ref, wgate_ref, wfin_ref, tgain_ref,
    out_ref,
    flag_all, right_all, left_send, left_all, tri_all, y_left, outer_buf, w_wide, w_perm, tri_buf,
    flag_ssem, flag_rsem, right_ssem, right_rsem, right_fsem, left_ssem, left_rsem,
    tri_ssem, tri_rsem, tri_fsem,
):
    n = nb * nz
    branch = lax.axis_index("branch")
    dap = lax.axis_index("dap")
    me = branch * nz + dap
    amino = aflag_ref.shape[1]
    seqs = hflag_ref.shape[1]
    rows = class_ref.shape[0]
    inner = wl_ref.shape[1]
    width = couple_ref.shape[1]
    reps = LANES // inner
    live = amino - 3 * amino // 8
    groups = live // reps
    pairs = rows * amino
    padded = -(-live // SUB) * SUB
    first = me * rows

    same = [(branch, lax.rem(dap + step, nz)) for step in range(1, nz)]
    here = [(lax.rem(branch + step, nb), dap) for step in range(1, nb)]
    far = [(b[0], z[1]) for b in here for z in same]
    near = same + here
    everyone = near + far

    def index_of(peer):
        return peer[0] * nz + peer[1]

    def target(peer):
        return {"branch": peer[0], "dap": peer[1]}

    barrier = pltpu.get_barrier_semaphore()
    for peer in everyone:
        pl.semaphore_signal(barrier, inc=1, device_id=target(peer), device_id_type=MESH)

    aflag = jnp.broadcast_to(aflag_ref[...].astype(F32), (SUB, amino)).astype(BF16)
    hflag32 = hflag_ref[...].astype(F32)
    hflag = jnp.broadcast_to(hflag32, (SUB, seqs)).astype(BF16)

    def lane_keys(lanes):
        r = iota((amino, lanes), 0)
        k = lax.rem(iota((amino, lanes), 1), amino)
        count = dot(aflag, (r <= k).astype(BF16))
        alive = dot(aflag, (r == k).astype(BF16))
        return (count * alive)[0:1, :]

    flag_all[me] = jnp.broadcast_to(jnp.sum(hflag32, axis=1, keepdims=True), (SUB, LANES))

    total = seqs * amino
    key_x = lane_keys(total)
    hlane = dot(hflag, (iota((seqs, total), 0) == iota((seqs, total), 1) // amino).astype(BF16))[0:1, :]
    key_x = jnp.where(hlane > 0.5, key_x, 0.0).astype(jnp.int32)
    m_row = iota((live * seqs, 1), 0)
    same_seq = lax.rem(m_row, seqs) == iota((1, total), 1) // amino
    gather_right = jnp.where((key_x == m_row // seqs + 1) & same_seq, 1.0, 0.0).astype(BF16)
    lane_group = iota((1, LANES), 1) // inner
    alane = dot(
        aflag,
        (iota((amino, amino * inner), 0) == iota((amino, amino * inner), 1) // inner).astype(BF16),
    )[0:1, :]

    normed = standardize(x_ref[...].astype(F32), hgain_ref[...]).astype(BF16)
    w_both = jnp.concatenate([wl_ref[...]] * reps + [wr_ref[...]] * reps, axis=1)
    sides = dot(normed, w_both)
    y_left[...] = sides[:, :LANES]
    right_rows = dot(gather_right, sides[:, LANES:].astype(BF16))
    for q in range(groups):
        block = right_rows[q * reps * seqs : (q * reps + 1) * seqs]
        for g in range(1, reps):
            start = (q * reps + g) * seqs
            block = jnp.where(lane_group == g, right_rows[start : start + seqs], block)
        right_all[me, :, q * LANES : (q + 1) * LANES] = block.astype(BF16)
    for d in range(n):
        block = y_left[pl.ds(d * rows, seqs, stride=amino), :]
        for g in range(1, rows):
            block = jnp.where(
                lane_group == g, y_left[pl.ds(d * rows + g, seqs, stride=amino), :], block
            )
        left_send[d] = (block * alane[:, d * LANES : (d + 1) * LANES]).astype(BF16)

    pl.semaphore_wait(barrier, n - 1)

    sends = []

    def push(src, dst, ssem, rsem, peer):
        copy = pltpu.make_async_remote_copy(
            src_ref=src, dst_ref=dst, send_sem=ssem, recv_sem=rsem,
            device_id=target(peer), device_id_type=MESH,
        )
        copy.start()
        sends.append(copy)

    def arrived(ref, slot, rsem):
        pltpu.make_async_remote_copy(
            src_ref=ref.at[slot], dst_ref=ref.at[slot], send_sem=rsem.at[slot],
            recv_sem=rsem.at[slot], device_id=target(everyone[0]), device_id_type=MESH,
        ).wait_recv()

    for peer in near:
        push(right_all.at[me], right_all.at[me], right_ssem.at[index_of(peer)], right_rsem.at[me], peer)
    for peer in everyone:
        d = index_of(peer)
        push(left_send.at[d], left_all.at[me], left_ssem.at[d], left_rsem.at[me], peer)
        push(flag_all.at[me], flag_all.at[me], flag_ssem.at[d], flag_rsem.at[me], peer)
    left_all[me] = left_send[me]

    w_wide[...] = wout_ref[...].astype(F32)
    for e in range(inner):
        w_perm[e * inner : (e + 1) * inner, :] = w_wide[
            pl.ds(e, inner, stride=inner), :
        ].astype(BF16)
    eye = iota((amino, amino), 0) == iota((amino, amino), 1)
    bins = embed_ref.shape[0]
    hot = []
    for i in range(rows):
        column = jnp.sum(
            jnp.where(eye, class_ref[i : i + 1, :], 0).astype(F32), axis=1, keepdims=True
        ).astype(jnp.int32)
        hot.append(jnp.where(column == iota((amino, bins), 1), 1.0, 0.0))
    onehot = jnp.concatenate(hot, axis=0).astype(BF16)
    base = couple_ref[...].astype(F32) + dot(onehot, embed_ref[...])

    key_pair = lane_keys(pairs)
    ilane = dot(
        aflag, (iota((amino, pairs), 0) == first + iota((amino, pairs), 1) // amino).astype(BF16)
    )[0:1, :]
    key_pair = jnp.where(ilane > 0.5, key_pair, 0.0).astype(jnp.int32)
    pair_row = iota((1, pairs), 1) // amino
    sel_rows = live * rows
    sel_m = iota((sel_rows, 1), 0)
    sel_key = key_pair == sel_m // rows + 1
    select_right = jnp.where(sel_key & (pair_row == lax.rem(sel_m, rows)), 1.0, 0.0).astype(BF16)
    select_left = jnp.concatenate(
        [jnp.where(sel_key & (pair_row == i), 1.0, 0.0) for i in range(rows)], axis=0
    ).astype(BF16)
    wide_key = jnp.broadcast_to(lane_keys(amino), (amino, amino))
    key_col = jnp.sum(jnp.where(eye, wide_key, 0.0), axis=1, keepdims=True).astype(jnp.int32)
    key_col = jnp.concatenate([key_col] * rows, axis=0)
    slots = rows * padded
    col = iota((pairs, slots), 1)
    expand = jnp.where(
        (key_col == lax.rem(col, padded) + 1) & (iota((pairs, slots), 0) // amino == col // padded),
        1.0,
        0.0,
    ).astype(BF16)
    expand = jnp.concatenate([expand, expand], axis=1)
    if padded > live:
        outer_buf[live * inner :, :] = jnp.zeros(((padded - live) * inner, LANES), F32)

    for peer in same:
        slot = index_of(peer)
        arrived(right_all, slot, right_rsem)
        for k, other in enumerate(here):
            push(right_all.at[slot], right_all.at[slot], right_fsem.at[k, peer[1]], right_rsem.at[slot], other)
    for peer in everyone:
        arrived(left_all, index_of(peer), left_rsem)
        arrived(flag_all, index_of(peer), flag_rsem)
    for peer in here + far:
        arrived(right_all, index_of(peer), right_rsem)

    number = jnp.maximum(jnp.sum(flag_all[...], axis=0)[0:1, :], 1.0)
    left = left_all[...].reshape(n * seqs, LANES)
    right = right_all[...].reshape(n * seqs, live * inner)
    outer_buf[: live * inner, :] = lax.dot_general(
        right, left, (((0,), (0,)), ((), ())), preferred_element_type=F32
    )
    parts = [[] for _ in range(rows)]
    lane = iota((1, LANES), 1)
    for q in range(inner // reps):
        block = [outer_buf[pl.ds(q * reps + g, padded, stride=inner), :] for g in range(reps)]
        span = reps // 2
        while span:
            upper = (lane // (span * inner)) % 2 == 1
            new = list(block)
            for a in range(reps):
                if a & span:
                    continue
                b = a | span
                shift = span * inner
                new[a] = jnp.where(upper, pltpu.roll(block[b], shift, 1), block[a])
                new[b] = jnp.where(upper, block[b], pltpu.roll(block[a], LANES - shift, 1))
            block = new
            span //= 2
        for i in range(rows):
            parts[i].append(block[i])
    packed = jnp.concatenate([jnp.concatenate(p, axis=1) for p in parts], axis=0).astype(BF16)
    product = dot(packed, w_perm[...])
    high = product.astype(BF16)
    low = (product - high.astype(F32)).astype(BF16)
    projected = dot(expand, jnp.concatenate([high, low], axis=0))
    updated = base + projected / number
    pair = standardize(updated, cgain_ref[...]).astype(BF16)
    right_two = dot(pair, wedge_ref[:, 2 * width :])
    tri_right = (jax.nn.sigmoid(right_two[:, :width]) * right_two[:, width:]).astype(BF16)
    tri_all[me] = dot(select_right, tri_right).astype(BF16)
    for peer in near:
        push(tri_all.at[me], tri_all.at[me], tri_ssem.at[index_of(peer)], tri_rsem.at[me], peer)

    left_two = dot(pair, wedge_ref[:, : 2 * width])
    tri_left = (jax.nn.sigmoid(left_two[:, :width]) * left_two[:, width:]).astype(BF16)
    spread_left = dot(select_left, tri_left)
    gate = jax.nn.sigmoid(dot(pair, wgate_ref[...]))

    for peer in same:
        slot = index_of(peer)
        arrived(tri_all, slot, tri_rsem)
        for k, other in enumerate(here):
            push(tri_all.at[slot], tri_all.at[slot], tri_fsem.at[k, peer[1]], tri_rsem.at[slot], other)
    for peer in here + far:
        arrived(tri_all, index_of(peer), tri_rsem)

    pieces = SUB // rows
    sub = iota((SUB, LANES), 0)
    for d in range(0, n, pieces):
        blocks = [tri_all[d + h].astype(F32) for h in range(pieces)]
        for i in range(rows):
            mine = spread_left[i * sel_rows : (i + 1) * sel_rows]
            result = None
            for h in range(pieces):
                both = mine * blocks[h]
                acc = jnp.sum(both.reshape(sel_rows // SUB, SUB, LANES), axis=0)
                step = rows
                while step < SUB:
                    acc = acc + pltpu.roll(acc, step, 0)
                    step *= 2
                result = acc if result is None else jnp.where(sub // rows == h, acc, result)
            tri_buf[i * amino + d * rows : i * amino + d * rows + SUB, :] = result
    tri = standardize(tri_buf[...], tgain_ref[...]).astype(BF16)
    out_ref[...] = (updated + gate * dot(tri, wfin_ref[...])).astype(BF16)
    for copy in sends:
        copy.wait_send()


def on_device(nb, nz, x, hflags, aflags, classes, couple, hgain, wl, wr, wout, embed, cgain, wedge, wgate, wfin, tgain):
    n = nb * nz
    seqs, amino, depth = x.shape
    rows, _, width = couple.shape
    inner = wl.shape[1]
    live = amino - 3 * amino // 8
    padded = -(-live // SUB) * SUB
    dma = pltpu.SemaphoreType.DMA
    operands = (
        x.reshape(seqs * amino, depth), hflags.reshape(1, seqs), aflags.reshape(1, amino), classes,
        couple.reshape(rows * amino, width), hgain.reshape(1, depth), wl, wr, wout, embed,
        cgain.reshape(1, width), wedge, wgate, wfin, tgain.reshape(1, width),
    )
    out = pl.pallas_call(
        functools.partial(kernel, nb, nz),
        out_shape=jax.ShapeDtypeStruct((rows * amino, width), BF16),
        in_specs=[pl.BlockSpec(memory_space=pltpu.VMEM)] * len(operands),
        out_specs=pl.BlockSpec(memory_space=pltpu.VMEM),
        scratch_shapes=[
            pltpu.VMEM((n, SUB, LANES), F32),
            pltpu.VMEM((n, seqs, live * inner), BF16),
            pltpu.VMEM((n, seqs, LANES), BF16),
            pltpu.VMEM((n, seqs, LANES), BF16),
            pltpu.VMEM((n, live * rows, width), BF16),
            pltpu.VMEM((seqs * amino, LANES), F32),
            pltpu.VMEM((padded * inner, LANES), F32),
            pltpu.VMEM((inner * inner, width), F32),
            pltpu.VMEM((inner * inner, width), BF16),
            pltpu.VMEM((rows * amino, width), F32),
            dma((n,)), dma((n,)),
            dma((n,)), dma((n,)), dma((nb, nz)),
            dma((n,)), dma((n,)),
            dma((n,)), dma((n,)), dma((nb, nz)),
        ],
        compiler_params=pltpu.CompilerParams(collective_id=0, has_side_effects=True),
    )(*operands)
    return out.reshape(rows, amino, width)


def solution(mesh):
    split = ("rep", "branch", "dap")
    placed = (
        P(split, None, None), P(split), P("rep"), P(split, None), P(split, None, None),
        P(), P(), P(), P(), P(), P(), P(), P(), P(), P(),
    )
    return jax.shard_map(
        functools.partial(on_device, mesh.shape["branch"], mesh.shape["dap"]),
        mesh=mesh,
        in_specs=placed,
        out_specs=P(split, None, None),
        check_vma=False,
    )
```

time: 98.2 us -> 22.9 us (0.23)
  blocking collectives: 72 us -> 0 us
  Pallas kernels: 0 us -> 19.1 us
  starting transfers between devices: 6.36 us -> 0 us
  other arithmetic: 5.91 us -> 0 us
  matrix products: 5.8 us -> 0 us
  local copies, waits for them, and re-layouts: 6.71 us -> 3.55 us
    all_gather x2 -> x0, blocking collectives: 54.8 us -> none  [the longest x1 29.4 us: on_device(): lax.all_gather(right_side, ('branch', 'dap'), axis=0, tiled=True)]
    pallas_call x0 -> x1, Pallas kernels: none -> 19.1 us  [on_device(): pl.pallas_call(functools.partial(kernel, nb, nz), out_shape=jax.ShapeDtyp...]
    unnamed x1 -> x0, blocking collectives: 17.2 us -> none
    all_to_all x1 -> x0, starting transfers between devices: 6.36 us -> none  [on_device(): lax.all_to_all(left_side, ('branch', 'dap'), split_axis=1, concat_axis=0,...]
    dot_general x8 -> x0, matrix products: 5.8 us -> none  [the longest x1 2.08 us: on_device(): jnp.einsum('sic,sje->ijce', left_rows, lax.all_gather(right_side, ('branc...]
    reduce_sum x6 -> x0, other arithmetic: 3.42 us -> none  [the longest x3 1.54 us: standardize_features(): spread = jnp.mean(centred * centred, axis=-1, keepdims=True)]
    transpose x1 -> x0, local copies, waits for them, and re-layouts: 1.93 us -> none  [on_device(): jnp.einsum('sic,sje->ijce', left_rows, lax.all_gather(right_side, ('branc...]
    unnamed x25 -> x5, local copies, waits for them, and re-layouts: 1.88 us -> 3.55 us
  transfers between devices with their start and end apart: 1 -> 0, of which waited for: 0 -> 0; matrix products, arithmetic and copies ran while one was open for 3% -> 0% of each run, Pallas kernels for 0% -> 0%
where the time goes in v1:
time: 22.9 us; the launch traced here: 22.6 us
  Pallas kernels  19.1 us (83%)
  local copies, waits for them, and re-layouts  3.55 us (16%)
    pallas_call x1, Pallas kernels, on_device(): pl.pallas_call(functools.partial(kernel, nb, nz), out_shape=jax.ShapeDtyp...  19.1 us
    unnamed x5, local copies, waits for them, and re-layouts  3.55 us

profile of v1, /device:TPU:0, one launch (start us, length us, event | category | flops | bytes accessed | tf_op | source)
XLA Modules:
  0.0 22.6 jit_solution(17671683625965891303)
XLA Ops:
  0.0 0.0 copy-start
  0.0 1.5 %copy.16.wl_ref = bf16[256,32]{1,0:T(8,128)(2,1)} copy(bf16[256,32]{0,1:T(8,128)(2,1)} %param.21) | data formatting | bytes 32768 | tf_op args[6]
  1.5 0.0 copy-done
  1.5 0.7 %copy.17.wr_ref = bf16[256,32]{1,0:T(8,128)(2,1)} copy(bf16[256,32]{0,1:T(8,128)(2,1)S(1)} %copy-done) | data formatting | bytes 32768 | tf_op args[7]
  2.2 19.1 %shard_map.145 = bf16[128,128]{1,0:T(8,128)(2,1)} custom-call(bf16[512,256]{1,0:T(8,128)(2,1)} %bitcast.8, s32[1,16]{1,0:T(1,128)} %bitcast.12, s32[1,32]{1,0:T(1,128)} %bitcast.13, s32[4,32]{1,0:T(4,128)} %class_ref.1, bf16[128,128]{1,0:T(8,128)(2,1)} %bitcast.10, f32[1,256]{1,0:T(1,128)} %bitcast.11, bf16[256,32]{1,0:T(8,128)(2,1)} %copy.16.wl_ref, ...), custom_call_target="tpu_custom_call" | custom-call | tf_op jit(solution)/shard_map/pallas_call | solution.py:284
  21.3 1.4 %copy.19 = bf16[4,32,128]{2,1,0:T(8,128)(2,1)} copy(bf16[4,32,128]{2,1,0:T(8,128)(2,1)} %bitcast.9) | data formatting | bytes 65536
Async XLA Ops:
  0.0 1.5 %copy-start = (bf16[256,32]{0,1:T(8,128)(2,1)S(1)}, bf16[256,32]{0,1:T(8,128)(2,1)}, u32[]{:S(2)}) copy-start(bf16[256,32]{0,1:T(8,128)(2,1)} %param.22) | copy-start | bytes 49156

commit v2 on v1

--- a/solution.py
+++ b/solution.py
@@ -45,7 +45,7 @@
     amino = aflag_ref.shape[1]
     seqs = hflag_ref.shape[1]
     rows = class_ref.shape[0]
-    inner = wl_ref.shape[1]
+    inner = wl_ref.shape[0]
     width = couple_ref.shape[1]
     reps = LANES // inner
     live = amino - 3 * amino // 8
@@ -97,8 +97,10 @@
     )[0:1, :]
 
     normed = standardize(x_ref[...].astype(F32), hgain_ref[...]).astype(BF16)
-    w_both = jnp.concatenate([wl_ref[...]] * reps + [wr_ref[...]] * reps, axis=1)
-    sides = dot(normed, w_both)
+    w_both = jnp.concatenate([wl_ref[...]] * reps + [wr_ref[...]] * reps, axis=0)
+    sides = lax.dot_general(
+        normed, w_both, (((1,), (1,)), ((), ())), preferred_element_type=F32
+    )
     y_left[...] = sides[:, :LANES]
     right_rows = dot(gather_right, sides[:, LANES:].astype(BF16))
     for q in range(groups):
@@ -278,12 +280,12 @@
     dma = pltpu.SemaphoreType.DMA
     operands = (
         x.reshape(seqs * amino, depth), hflags.reshape(1, seqs), aflags.reshape(1, amino), classes,
-        couple.reshape(rows * amino, width), hgain.reshape(1, depth), wl, wr, wout, embed,
+        couple.reshape(rows * amino, width), hgain.reshape(1, depth), wl.T, wr.T, wout, embed,
         cgain.reshape(1, width), wedge, wgate, wfin, tgain.reshape(1, width),
     )
     out = pl.pallas_call(
         functools.partial(kernel, nb, nz),
-        out_shape=jax.ShapeDtypeStruct((rows * amino, width), BF16),
+        out_shape=pltpu.VMEM((rows * amino, width), BF16),
         in_specs=[pl.BlockSpec(memory_space=pltpu.VMEM)] * len(operands),
         out_specs=pl.BlockSpec(memory_space=pltpu.VMEM),
         scratch_shapes=[

time: 22.9 us -> 19.2 us (0.84)
  local copies, waits for them, and re-layouts: 3.55 us -> 0.62 us
  Pallas kernels: 19.1 us -> 18.4 us
    unnamed x5 -> x1, local copies, waits for them, and re-layouts: 3.55 us -> 0.62 us
    pallas_call x1, Pallas kernels: 19.1 us -> 18.4 us  [on_device(): pl.pallas_call(functools.partial(kernel, nb, nz), out_shape=pltpu.VMEM((r...]
where the time goes in v2:
time: 19.2 us; the launch traced here: 19.1 us
  Pallas kernels  18.4 us (96%)
  local copies, waits for them, and re-layouts  0.62 us (3%)
    pallas_call x1, Pallas kernels, on_device(): pl.pallas_call(functools.partial(kernel, nb, nz), out_shape=pltpu.VMEM((r...  18.4 us
    unnamed x1, local copies, waits for them, and re-layouts  0.62 us

profile of v2, /device:TPU:0, one launch (start us, length us, event | category | flops | bytes accessed | tf_op | source)
XLA Modules:
  0.0 19.1 jit_solution(9294207538556942141)
XLA Ops:
  0.0 18.4 %shard_map.145 = bf16[128,128]{1,0:T(8,128)(2,1)S(1)} custom-call(bf16[512,256]{1,0:T(8,128)(2,1)} %bitcast.11, s32[1,16]{1,0:T(1,128)} %bitcast.16, s32[1,32]{1,0:T(1,128)} %bitcast.17, s32[4,32]{1,0:T(4,128)} %class_ref.1, bf16[128,128]{1,0:T(8,128)(2,1)} %bitcast.12, f32[1,256]{1,0:T(1,128)} %bitcast.15, bf16[32,256]{1,0:T(8,128)(2,1)} %bitcast.13, ...), custom_call_target="tpu_custom_call" | custom-call | tf_op jit(solution)/shard_map/pallas_call | solution.py:286
  18.4 0.6 %copy.17 = bf16[4,32,128]{2,1,0:T(8,128)(2,1)} copy(bf16[4,32,128]{2,1,0:T(8,128)(2,1)S(1)} %bitcast.10) | data formatting | bytes 65536

commit v3 on v2

--- a/solution.py
+++ b/solution.py
@@ -10,6 +10,7 @@
 F32 = jnp.float32
 BF16 = jnp.bfloat16
 MESH = pl.DeviceIdType.MESH
+OPERANDS = 15
 LANES = 128
 SUB = 8
 
@@ -31,13 +32,17 @@
 
 def kernel(
     nb, nz,
-    x_ref, hflag_ref, aflag_ref, class_ref, couple_ref, hgain_ref, wl_ref, wr_ref, wout_ref,
-    embed_ref, cgain_ref, wedge_ref, wgate_ref, wfin_ref, tgain_ref,
-    out_ref,
+    *refs,
+):
+    operands, out_ref, held = refs[:OPERANDS], refs[OPERANDS], refs[OPERANDS + 1 : 2 * OPERANDS + 1]
+    in_sem, *scratch = refs[2 * OPERANDS + 1 :]
+    (x_ref, hflag_ref, aflag_ref, class_ref, couple_ref, hgain_ref, wl_ref, wr_ref, wout_ref,
+     embed_ref, cgain_ref, wedge_ref, wgate_ref, wfin_ref, tgain_ref) = held
+    (
     flag_all, right_all, left_send, left_all, tri_all, y_left, outer_buf, w_wide, w_perm, tri_buf,
     flag_ssem, flag_rsem, right_ssem, right_rsem, right_fsem, left_ssem, left_rsem,
     tri_ssem, tri_rsem, tri_fsem,
-):
+    ) = scratch
     n = nb * nz
     branch = lax.axis_index("branch")
     dap = lax.axis_index("dap")
@@ -70,6 +75,13 @@
     for peer in everyone:
         pl.semaphore_signal(barrier, inc=1, device_id=target(peer), device_id_type=MESH)
 
+    loads = {}
+    for k in (2, 1, 0, 5, 6, 7, 8, 3, 4, 9, 10, 11, 12, 13, 14):
+        loads[k] = pltpu.make_async_copy(operands[k], held[k], in_sem.at[k])
+        loads[k].start()
+
+    loads[2].wait()
+    loads[1].wait()
     aflag = jnp.broadcast_to(aflag_ref[...].astype(F32), (SUB, amino)).astype(BF16)
     hflag32 = hflag_ref[...].astype(F32)
     hflag = jnp.broadcast_to(hflag32, (SUB, seqs)).astype(BF16)
@@ -81,7 +93,7 @@
         alive = dot(aflag, (r == k).astype(BF16))
         return (count * alive)[0:1, :]
 
-    flag_all[me] = jnp.broadcast_to(jnp.sum(hflag32, axis=1, keepdims=True), (SUB, LANES))
+    flag_all[me] = jnp.broadcast_to(jnp.sum(hflag32, axis=1, keepdims=True), (1, LANES))
 
     total = seqs * amino
     key_x = lane_keys(total)
@@ -96,6 +108,8 @@
         (iota((amino, amino * inner), 0) == iota((amino, amino * inner), 1) // inner).astype(BF16),
     )[0:1, :]
 
+    for k in (0, 5, 6, 7):
+        loads[k].wait()
     normed = standardize(x_ref[...].astype(F32), hgain_ref[...]).astype(BF16)
     w_both = jnp.concatenate([wl_ref[...]] * reps + [wr_ref[...]] * reps, axis=0)
     sides = lax.dot_general(
@@ -135,14 +149,18 @@
             recv_sem=rsem.at[slot], device_id=target(everyone[0]), device_id_type=MESH,
         ).wait_recv()
 
+    for peer in everyone:
+        d = index_of(peer)
+        push(flag_all.at[me], flag_all.at[me], flag_ssem.at[d], flag_rsem.at[me], peer)
     for peer in near:
         push(right_all.at[me], right_all.at[me], right_ssem.at[index_of(peer)], right_rsem.at[me], peer)
     for peer in everyone:
         d = index_of(peer)
         push(left_send.at[d], left_all.at[me], left_ssem.at[d], left_rsem.at[me], peer)
-        push(flag_all.at[me], flag_all.at[me], flag_ssem.at[d], flag_rsem.at[me], peer)
     left_all[me] = left_send[me]
 
+    for k in (8, 3, 4, 9, 10, 11, 12, 13, 14):
+        loads[k].wait()
     w_wide[...] = wout_ref[...].astype(F32)
     for e in range(inner):
         w_perm[e * inner : (e + 1) * inner, :] = w_wide[
@@ -197,7 +215,7 @@
     for peer in here + far:
         arrived(right_all, index_of(peer), right_rsem)
 
-    number = jnp.maximum(jnp.sum(flag_all[...], axis=0)[0:1, :], 1.0)
+    number = jnp.maximum(jnp.sum(flag_all[...], axis=0), 1.0)
     left = left_all[...].reshape(n * seqs, LANES)
     right = right_all[...].reshape(n * seqs, live * inner)
     outer_buf[: live * inner, :] = lax.dot_general(
@@ -286,10 +304,12 @@
     out = pl.pallas_call(
         functools.partial(kernel, nb, nz),
         out_shape=pltpu.VMEM((rows * amino, width), BF16),
-        in_specs=[pl.BlockSpec(memory_space=pltpu.VMEM)] * len(operands),
+        in_specs=[pl.BlockSpec(memory_space=pl.ANY)] * OPERANDS,
         out_specs=pl.BlockSpec(memory_space=pltpu.VMEM),
-        scratch_shapes=[
-            pltpu.VMEM((n, SUB, LANES), F32),
+        scratch_shapes=[pltpu.VMEM(a.shape, a.dtype) for a in operands]
+        + [
+            dma((OPERANDS,)),
+            pltpu.VMEM((n, 1, LANES), F32),
             pltpu.VMEM((n, seqs, live * inner), BF16),
             pltpu.VMEM((n, seqs, LANES), BF16),
             pltpu.VMEM((n, seqs, LANES), BF16),

time: 19.2 us -> 17.9 us (0.932)
  Pallas kernels: 18.4 us -> 17.1 us
    pallas_call x1, Pallas kernels: 18.4 us -> 17.1 us  [on_device(): pl.pallas_call(functools.partial(kernel, nb, nz), out_shape=pltpu.VMEM((r...]
where the time goes in v3:
time: 17.9 us; the launch traced here: 17.8 us
  Pallas kernels  17.1 us (96%)
  local copies, waits for them, and re-layouts  0.62 us (3%)
    pallas_call x1, Pallas kernels, on_device(): pl.pallas_call(functools.partial(kernel, nb, nz), out_shape=pltpu.VMEM((r...  17.1 us
    unnamed x1, local copies, waits for them, and re-layouts  0.62 us

profile of v3, /device:TPU:0, one launch (start us, length us, event | category | flops | bytes accessed | tf_op | source)
XLA Modules:
  0.0 17.8 jit_solution(8218106408423832012)
XLA Ops:
  0.0 17.1 %shard_map.145 = bf16[128,128]{1,0:T(8,128)(2,1)S(1)} custom-call(bf16[512,256]{1,0:T(8,128)(2,1)} %bitcast.11, s32[1,16]{1,0:T(1,128)} %bitcast.16, s32[1,32]{1,0:T(1,128)} %bitcast.17, s32[4,32]{1,0:T(4,128)} %refs_3_.1, bf16[128,128]{1,0:T(8,128)(2,1)} %bitcast.12, f32[1,256]{1,0:T(1,128)} %bitcast.15, bf16[32,256]{1,0:T(8,128)(2,1)} %bitcast.13, ...), custom_call_target="tpu_custom_call" | custom-call | tf_op jit(solution)/shard_map/pallas_call | solution.py:304
  17.1 0.6 %copy.17 = bf16[4,32,128]{2,1,0:T(8,128)(2,1)} copy(bf16[4,32,128]{2,1,0:T(8,128)(2,1)S(1)} %bitcast.10) | data formatting | bytes 65536

commit v4 on v3

--- a/solution.py
+++ b/solution.py
@@ -258,18 +258,17 @@
     spread_left = dot(select_left, tri_left)
     gate = jax.nn.sigmoid(dot(pair, wgate_ref[...]))
 
-    for peer in same:
+    def passing(peer):
         slot = index_of(peer)
         arrived(tri_all, slot, tri_rsem)
         for k, other in enumerate(here):
             push(tri_all.at[slot], tri_all.at[slot], tri_fsem.at[k, peer[1]], tri_rsem.at[slot], other)
-    for peer in here + far:
-        arrived(tri_all, index_of(peer), tri_rsem)
 
     pieces = SUB // rows
     sub = iota((SUB, LANES), 0)
-    for d in range(0, n, pieces):
-        blocks = [tri_all[d + h].astype(F32) for h in range(pieces)]
+
+    def triangle(start):
+        blocks = [tri_all[start + h].astype(F32) for h in range(pieces)]
         for i in range(rows):
             mine = spread_left[i * sel_rows : (i + 1) * sel_rows]
             result = None
@@ -281,7 +280,24 @@
                     acc = acc + pltpu.roll(acc, step, 0)
                     step *= 2
                 result = acc if result is None else jnp.where(sub // rows == h, acc, result)
-            tri_buf[i * amino + d * rows : i * amino + d * rows + SUB, :] = result
+            row = i * amino + start * rows
+            tri_buf[pl.ds(row if isinstance(row, int) else pl.multiple_of(row, SUB), SUB), :] = result
+
+    for peer in same:
+        passing(peer)
+    if nz % pieces == 0:
+        for b in [branch] + [o[0] for o in here]:
+            if b is not branch:
+                for peer in here + far:
+                    if peer[0] is b:
+                        arrived(tri_all, index_of(peer), tri_rsem)
+            for z in range(0, nz, pieces):
+                triangle(b * nz + z)
+    else:
+        for peer in here + far:
+            arrived(tri_all, index_of(peer), tri_rsem)
+        for d in range(0, n, pieces):
+            triangle(d)
     tri = standardize(tri_buf[...], tgain_ref[...]).astype(BF16)
     out_ref[...] = (updated + gate * dot(tri, wfin_ref[...])).astype(BF16)
     for copy in sends:

time: 17.9 us -> 17.9 us (level)
  no operation moved by 1% of the time
where the time goes in v4:
time: 17.9 us; the launch traced here: 17.7 us
  Pallas kernels  17.1 us (96%)
  local copies, waits for them, and re-layouts  0.62 us (3%)
    pallas_call x1, Pallas kernels, on_device(): pl.pallas_call(functools.partial(kernel, nb, nz), out_shape=pltpu.VMEM((r...  17.1 us
    unnamed x1, local copies, waits for them, and re-layouts  0.62 us

profile of v4, /device:TPU:0, one launch (start us, length us, event | category | flops | bytes accessed | tf_op | source)
XLA Modules:
  0.0 17.7 jit_solution(2384967582824454417)
XLA Ops:
  0.0 17.1 %shard_map.145 = bf16[128,128]{1,0:T(8,128)(2,1)S(1)} custom-call(bf16[512,256]{1,0:T(8,128)(2,1)} %bitcast.11, s32[1,16]{1,0:T(1,128)} %bitcast.16, s32[1,32]{1,0:T(1,128)} %bitcast.17, s32[4,32]{1,0:T(4,128)} %refs_3_.1, bf16[128,128]{1,0:T(8,128)(2,1)} %bitcast.12, f32[1,256]{1,0:T(1,128)} %bitcast.15, bf16[32,256]{1,0:T(8,128)(2,1)} %bitcast.13, ...), custom_call_target="tpu_custom_call" | custom-call | tf_op jit(solution)/shard_map/pallas_call | solution.py:320
  17.1 0.6 %copy.17 = bf16[4,32,128]{2,1,0:T(8,128)(2,1)} copy(bf16[4,32,128]{2,1,0:T(8,128)(2,1)S(1)} %bitcast.10) | data formatting | bytes 65536
